TPU v7x, 256 devices: a whole 4x4x8 slice. The times are simulated.
256 devices in a mesh: src: 4 (over x), space: 64 (over z, y, core).
Axes of the slice: x: 4, y: 4, z: 8, core: 2. Of those that a mesh axis runs over, the one named last changes fastest.
Arguments:
- contrast: float32 [2, 64, 256, 256], P(None, None, 'space'), may hold values from -0.4 to 0.45
- measured: float32 [4, 2, 256, 256], P('src', None, 'space'), may hold values from -7 to 7
- positions: int32 [4, 2], P('src'), may hold values from 0 to 255
Outputs:
- contrast_sources: float32 [4, 2, 64, 256, 256], P('src', None, None, 'space')
- contrast_new: float32 [2, 64, 256, 256], P(None, None, 'space')
All inputs are finite; a program needn't handle non-finite values.
Results may differ from a plain program's by a relative error of at most 0.0003.
Values sent between devices are 32-bit elements; how exact they have to be, the bound alone decides.
A program may use at most 64 MiB of HBM per device.

v0:
```python
from functools import partial
import math
import jax
import jax.numpy as jnp
from jax import lax
from jax.sharding import PartitionSpec as P

NX = 256
NY = 256
NZ = 64
OUTER = 2
WAVENUMBER = 2.0 * math.pi / 6.0
DAMPING = 0.3
SOURCE_GAP = 8.0
FLOOR_SHARE = 0.75
REAL_LOW = -0.25
REAL_HIGH = 0.35
IMAG_HIGH = 0.1
DEPTH_PATTERN = "akbn,sbnxy->sakxy"
FIRST_PATTERN = "akbn,sbznj->sazkj"
SECOND_PATTERN = "akbn,sbzxn->sazxk"


def laplace_modes(start_mode, length, total):
    mode_index = (start_mode + jnp.arange(length)).astype(jnp.float32)
    half_sine = jnp.sin(math.pi * mode_index / total)
    return 4.0 * half_sine * half_sine


def green_spectrum(depth_modes, first_modes, second_modes):
    eigen = depth_modes[:, None, None] + first_modes[None, :, None] + second_modes[None, None, :]
    wave_sq = WAVENUMBER * WAVENUMBER
    real_den = eigen - wave_sq
    imag_den = wave_sq * DAMPING
    factor = wave_sq / (real_den * real_den + imag_den * imag_den)
    return (factor * real_den, factor * imag_den)


def incident(positions, start_row, row_count):
    heights = jnp.arange(NZ).astype(jnp.float32) + SOURCE_GAP
    across = (start_row + jnp.arange(row_count)).astype(jnp.float32)
    along_y = jnp.arange(NY).astype(jnp.float32)
    source_x = positions[:, 0].astype(jnp.float32)
    source_y = positions[:, 1].astype(jnp.float32)
    offset_x = across[None, :] - source_x[:, None]
    offset_y = along_y[None, :] - source_y[:, None]
    dist_sq = (
        heights[None, :, None, None] * heights[None, :, None, None]
        + offset_x[:, None, :, None] * offset_x[:, None, :, None]
    )
    dist_sq = dist_sq + offset_y[:, None, None, :] * offset_y[:, None, None, :]
    phases = WAVENUMBER * jnp.sqrt(dist_sq)
    return (jnp.cos(phases), jnp.sin(phases))


def dft_table(length, orient, factor):
    indices = jnp.arange(length)
    turn_index = indices[:, None] * indices[None, :] % length
    angles = 2.0 * math.pi / length * turn_index.astype(jnp.float32)
    cosine = jnp.cos(angles) * factor
    sine_part = orient * jnp.sin(angles) * factor
    upper_rows = jnp.stack([cosine, sine_part], axis=1)
    bottom = jnp.stack([-sine_part, cosine], axis=1)
    return jnp.stack([upper_rows, bottom], axis=0)


def apply_table(table, fields, pattern):
    return jnp.einsum(pattern, table, fields, precision=lax.Precision.HIGHEST)


def times_green(spectrum, green_real, green_imag):
    real_part = spectrum[:, 0] * green_real - spectrum[:, 1] * green_imag
    imag_part = spectrum[:, 0] * green_imag + spectrum[:, 1] * green_real
    return jnp.stack([real_part, imag_part], axis=1)


def transform(fields, spectral, tables):
    z_forward, x_forward, y_forward, z_inverse, x_inverse, y_inverse = tables
    depth_done = apply_table(z_forward, fields, DEPTH_PATTERN)
    planes = apply_table(
        x_forward,
        lax.all_to_all(depth_done, "space", split_axis=2, concat_axis=3, tiled=True),
        FIRST_PATTERN,
    )
    spectrum = spectral(apply_table(y_forward, planes, SECOND_PATTERN))
    returned = apply_table(
        x_inverse, apply_table(y_inverse, spectrum, SECOND_PATTERN), FIRST_PATTERN
    )
    return apply_table(
        z_inverse,
        lax.all_to_all(returned, "space", split_axis=3, concat_axis=2, tiled=True),
        DEPTH_PATTERN,
    )


def descent_total(descent):
    local_sum = jnp.sum(descent * descent)
    return lax.psum(local_sum, ("src", "space"))


def bounded(numerator, power_sum, total_sources):
    floored = jnp.maximum(power_sum, FLOOR_SHARE * total_sources)
    return jnp.stack(
        [
            jnp.clip(numerator[0] / floored, REAL_LOW, REAL_HIGH),
            jnp.clip(numerator[1] / floored, 0.0, IMAG_HIGH),
        ],
        axis=0,
    )


def on_device(contrast, measured, positions):
    spaces = lax.axis_size("space")
    sources = positions.shape[0]
    row_count = contrast.shape[2]
    plane_count = NZ // spaces
    start_row = lax.axis_index("space") * row_count
    total_sources = sources * lax.axis_size("src")
    chi_real, chi_imag = (contrast[0], contrast[1])
    inc_real, inc_imag = incident(positions, start_row, row_count)
    tables = (
        dft_table(NZ, 1.0, 1.0),
        dft_table(NX, 1.0, 1.0),
        dft_table(NY, 1.0, 1.0),
        dft_table(NZ, -1.0, 1.0 / NZ),
        dft_table(NX, -1.0, 1.0 / NX),
        dft_table(NY, -1.0, 1.0 / NY),
    )
    green_real, green_imag = green_spectrum(
        laplace_modes(lax.axis_index("space") * plane_count, plane_count, NZ),
        laplace_modes(0, NX, NX),
        laplace_modes(0, NY, NY),
    )
    forward_green = partial(times_green, green_real=green_real, green_imag=green_imag)
    adjoint_green = partial(times_green, green_real=green_real, green_imag=-green_imag)
    sources_field = jnp.stack(
        [chi_real * inc_real - chi_imag * inc_imag, chi_real * inc_imag + chi_imag * inc_real],
        axis=1,
    )
    scattered = transform(sources_field, forward_green, tables)
    data_real = measured[:, 0]
    data_imag = measured[:, 1]
    data_local = jnp.sum(data_real * data_real + data_imag * data_imag)
    for outer_step in range(OUTER):
        chi_inc_real = chi_real * inc_real - chi_imag * inc_imag
        chi_inc_imag = chi_real * inc_imag + chi_imag * inc_real
        object_local = jnp.sum(chi_inc_real * chi_inc_real + chi_inc_imag * chi_inc_imag)
        data_total, object_total = lax.psum((data_local, object_local), ("src", "space"))
        data_weight = 1.0 / data_total
        object_weight = 1.0 / object_total
        total_real = inc_real + scattered[:, 0]
        total_imag = inc_imag + scattered[:, 1]
        resid_real = chi_real * total_real - chi_imag * total_imag - sources_field[:, 0]
        resid_imag = chi_real * total_imag + chi_imag * total_real - sources_field[:, 1]
        adjoint_real = -object_weight * (chi_real * resid_real + chi_imag * resid_imag)
        adjoint_imag = -object_weight * (chi_real * resid_imag - chi_imag * resid_real)
        adjoint_real = adjoint_real.at[:, 0].add(data_weight * (data_real - scattered[:, 0, 0]))
        adjoint_imag = adjoint_imag.at[:, 0].add(data_weight * (data_imag - scattered[:, 1, 0]))
        adjoint_input = jnp.stack([adjoint_real, adjoint_imag], axis=1)
        residual = jnp.stack([resid_real, resid_imag], axis=1)
        adjoint_image = transform(adjoint_input, adjoint_green, tables)
        descent = object_weight * residual + adjoint_image
        descent_early = descent_total(descent)
        descent_image = transform(descent, forward_green, tables)
        image_real = descent_image[:, 0]
        image_imag = descent_image[:, 1]
        change_real = descent[:, 0] - (chi_real * image_real - chi_imag * image_imag)
        change_imag = descent[:, 1] - (chi_real * image_imag + chi_imag * image_real)
        image_local = jnp.sum(
            image_real[:, 0] * image_real[:, 0] + image_imag[:, 0] * image_imag[:, 0]
        )
        change_local = jnp.sum(change_real * change_real + change_imag * change_imag)
        image_total, change_total = lax.psum((image_local, change_local), ("src", "space"))
        step_length = descent_early / (data_weight * image_total + object_weight * change_total)
        sources_field = sources_field + step_length * descent
        scattered = scattered + step_length * descent_image
        total_real = inc_real + scattered[:, 0]
        total_imag = inc_imag + scattered[:, 1]
        numerator_real = jnp.sum(
            sources_field[:, 0] * total_real + sources_field[:, 1] * total_imag, axis=0
        )
        numerator_imag = jnp.sum(
            sources_field[:, 1] * total_real - sources_field[:, 0] * total_imag, axis=0
        )
        power_sum = jnp.sum(total_real * total_real + total_imag * total_imag, axis=0)
        numerator = jnp.stack([numerator_real, numerator_imag], axis=0)
        numerator_all, power_all = lax.psum((numerator, power_sum), "src")
        contrast_now = bounded(numerator_all, power_all, total_sources)
        chi_real = contrast_now[0]
        chi_imag = contrast_now[1]
    return (sources_field, contrast_now)


def solution(mesh):
    placed = (P(None, None, "space", None), P("src", None, "space", None), P("src", None))
    return jax.shard_map(
        on_device,
        mesh=mesh,
        in_specs=placed,
        out_specs=(P("src", None, None, "space", None), P(None, None, "space", None)),
        check_vma=False,
    )
```

profile of v0, /device:TPU:8, one launch (start us, length us, event | category | flops | bytes accessed | tf_op | source)
XLA Modules:
  0.0 783.4 jit_solution(12502016712081461501)
XLA Ops:
  10.4 6.7 copy_cosine_fusion
  17.2 3.5 add_reduce_fusion.1
  22.7 13.0 %all-to-all-start = ((f32[1,2,64,4,256]{4,1,3,0,2:T(2,128)}), f32[1,2,64,4,256]{4,1,3,0,2:T(2,128)}, u32[]{:S(2)}, u32[]{:S(2)}) async-start(f32[1,2,64,4,256]{4,1,3,0,2:T(2,128)} %copy.363), calls=%async_computation | async-start | bytes 1048576 | tf_op jit(solution)/shard_map/all_to_all | solution.py:82
  40.1 12.9 %all-to-all-done = f32[1,2,64,4,256]{4,1,3,0,2:T(2,128)} async-done(((f32[1,2,64,4,256]{4,1,3,0,2:T(2,128)}), f32[1,2,64,4,256]{4,1,3,0,2:T(2,128)}, u32[]{:S(2)}, u32[]{:S(2)}) %all-to-all-start) | async-done | bytes 524320 | tf_op jit(solution)/shard_map/all_to_all | solution.py:82
  53.0 2.0 copy.364
  55.0 2.1 convolution_bitcast_fusion.28
  57.1 1.9 convolution_bitcast_fusion.27
  60.2 2.7 convolution_bitcast_fusion.25
  62.9 2.0 copy.367
  64.9 6.1 all-to-all-start.1
  71.0 2.0 fusion.119
  73.0 76.7 %all-reduce.2 = (f32[]{:T(128)}, f32[]{:T(128)}) all-reduce(f32[]{:T(128)} %get-tuple-element.82, f32[]{:T(128)} %get-tuple-element.133), channel_id=1, replica_groups=mesh['src'=4,'space'=64] {'src','space'}, use_global_device_ids=true, to_apply=%region_1.2 | all-reduce | flops 2 | bytes 16 | tf_op jit(solution)/shard_map/psum | solution.py:148
  154.8 7.7 add_multiply_fusion.1
  165.8 26.7 %all_to_all.40 = f32[1,2,64,4,256]{4,1,3,0,2:T(2,128)S(1)} all-to-all(f32[1,2,64,4,256]{4,1,3,0,2:T(2,128)S(1)} %copy.380), channel_id=1, replica_groups=mesh['src'=4,'space'=64] {'space'}, dimensions={2} | all-to-all | bytes 1048576 | tf_op jit(solution)/shard_map/all_to_all | solution.py:82
  193.8 1.9 convolution_bitcast_fusion.21
  197.0 1.9 convolution_bitcast_fusion.19
  199.8 6.2 all-to-all-start.3
  207.8 15.7 %all-to-all-done.3 = f32[1,2,1,256,256]{4,1,2,0,3:T(2,128)} async-done(((f32[1,2,1,256,256]{4,1,2,0,3:T(2,128)}), f32[1,2,1,256,256]{4,1,2,0,3:T(2,128)}, u32[]{:S(2)}, u32[]{:S(2)}) %all-to-all-start.3) | async-done | bytes 524320 | tf_op jit(solution)/shard_map/all_to_all | solution.py:91
  227.5 23.7 %all_to_all.41 = f32[1,2,64,4,256]{4,1,3,0,2:T(2,128)} all-to-all(f32[1,2,64,4,256]{4,1,3,0,2:T(2,128)S(1)} %copy.388), channel_id=1, replica_groups=mesh['src'=4,'space'=64] {'space'}, dimensions={2} | all-to-all | bytes 1048576 | tf_op jit(solution)/shard_map/all_to_all | solution.py:82
  251.2 2.0 copy.389
  253.3 2.1 convolution_bitcast_fusion.16
  255.4 1.9 convolution_bitcast_fusion.15
  258.5 2.7 convolution_bitcast_fusion.13
  261.2 2.0 copy.392
  263.2 6.1 all-to-all-start.5
  270.2 16.6 %all-to-all-done.5 = f32[1,2,1,256,256]{4,1,2,0,3:T(2,128)} async-done(((f32[1,2,1,256,256]{4,1,2,0,3:T(2,128)}), f32[1,2,1,256,256]{4,1,2,0,3:T(2,128)}, u32[]{:S(2)}, u32[]{:S(2)}) %all-to-all-start.5) | async-done | bytes 524320 | tf_op jit(solution)/shard_map/all_to_all | solution.py:91
  291.7 73.1 %all-reduce.1 = (f32[]{:T(128)}, f32[]{:T(128)}, f32[]{:T(128)}) all-reduce(f32[]{:T(128)} %get-tuple-element.77, f32[]{:T(128)} %fusion.95, f32[]{:T(128)} %fusion.62), channel_id=1, replica_groups=mesh['src'=4,'space'=64] {'src','space'}, use_global_device_ids=true, to_apply=%region_5.6 | all-reduce | flops 3 | bytes 24 | tf_op jit(solution)/shard_map/psum | solution.py:98
  369.6 3.2 fusion.56
  372.8 2.3 fusion.49
  376.1 45.6 %all-reduce.10.cloned.1.call-done = (f32[2,64,4,256]{3,2,1,0:T(4,128)}, f32[64,4,256]{2,1,0:T(4,128)}) async-done(((f32[2,64,4,256]{3,2,1,0:T(4,128)}, f32[64,4,256]{2,1,0:T(4,128)}), (f32[2,64,4,256]{3,2,1,0:T(4,128)}, f32[64,4,256]{2,1,0:T(4,128)})) %all-reduce.10.cloned.1.call-update) | async-done | bytes 786448 | tf_op jit(solution)/shard_map/psum | solution.py:187
  424.5 3.3 add_reduce_fusion
  429.2 74.8 %psum.101 = f32[]{:T(128)} all-reduce(f32[]{:T(128)} %add_reduce_fusion), channel_id=1, replica_groups=mesh['src'=4,'space'=64] {'src','space'}, use_global_device_ids=true, to_apply=%region_13.14 | all-reduce | flops 1 | bytes 8 | tf_op jit(solution)/shard_map/psum | solution.py:148
  504.5 4.0 add_multiply_fusion
  512.7 26.4 %all_to_all.42 = f32[1,2,64,4,256]{4,1,3,0,2:T(2,128)} all-to-all(f32[1,2,64,4,256]{4,1,3,0,2:T(2,128)S(1)} %copy.427), channel_id=1, replica_groups=mesh['src'=4,'space'=64] {'space'}, dimensions={2} | all-to-all | bytes 1048576 | tf_op jit(solution)/shard_map/all_to_all | solution.py:82
  541.4 1.9 convolution_bitcast_fusion.9
  544.6 1.9 convolution_bitcast_fusion.7
  547.4 6.2 all-to-all-start.7
  555.6 15.5 %all-to-all-done.7 = f32[1,2,1,256,256]{4,1,2,0,3:T(2,128)} async-done(((f32[1,2,1,256,256]{4,1,2,0,3:T(2,128)}), f32[1,2,1,256,256]{4,1,2,0,3:T(2,128)}, u32[]{:S(2)}, u32[]{:S(2)}) %all-to-all-start.7) | async-done | bytes 524320 | tf_op jit(solution)/shard_map/all_to_all | solution.py:91
  575.9 23.7 %all_to_all.43 = f32[1,2,64,4,256]{4,1,3,0,2:T(2,128)} all-to-all(f32[1,2,64,4,256]{4,1,3,0,2:T(2,128)S(1)} %copy.435), channel_id=1, replica_groups=mesh['src'=4,'space'=64] {'space'}, dimensions={2} | all-to-all | bytes 1048576 | tf_op jit(solution)/shard_map/all_to_all | solution.py:82
  599.6 2.0 copy.436
  601.6 2.1 convolution_bitcast_fusion.4
  603.7 1.9 convolution_bitcast_fusion.3
  609.8 5.9 all-to-all-start.9
  616.1 17.1 %all-to-all-done.9 = f32[1,2,1,256,256]{4,1,2,0,3:T(2,128)S(1)} async-done(((f32[1,2,1,256,256]{4,1,2,0,3:T(2,128)}), f32[1,2,1,256,256]{4,1,2,0,3:T(2,128)S(1)}, u32[]{:S(2)}, u32[]{:S(2)}) %all-to-all-start.9) | async-done | bytes 524320 | tf_op jit(solution)/shard_map/all_to_all | solution.py:91
  636.9 73.1 %all-reduce = (f32[]{:T(128)}, f32[]{:T(128)}, f32[]{:T(128)}) all-reduce(f32[]{:T(128)} %get-tuple-element.72, f32[]{:T(128)} %fusion.96, f32[]{:T(128)} %fusion.44), channel_id=1, replica_groups=mesh['src'=4,'space'=64] {'src','space'}, use_global_device_ids=true, to_apply=%region_15.16 | all-reduce | flops 3 | bytes 24 | tf_op jit(solution)/shard_map/psum | solution.py:98
  714.6 2.1 fusion.41
  718.8 7.3 multiply_add_fusion.1
  728.3 44.7 %all-reduce.8.cloned.1.call-done = (f32[2,64,4,256]{3,0,2,1:T(2,128)}, f32[64,4,256]{2,0,1:T(8,128)}) async-done(((f32[2,64,4,256]{3,0,2,1:T(2,128)}, f32[64,4,256]{2,0,1:T(8,128)}), (f32[2,64,4,256]{3,0,2,1:T(2,128)}, f32[64,4,256]{2,0,1:T(8,128)})) %all-reduce.8.cloned.1.call-update) | async-done | bytes 786448 | tf_op jit(solution)/shard_map/psum | solution.py:187
  (210 shorter events, 73.9 us)
Async XLA Ops:
  7.2 10.0 %copy-start.44 = (f32[2,64,4,256]{3,2,1,0:T(4,128)S(1)}, f32[2,64,4,256]{3,2,1,0:T(4,128)}, u32[]{:S(2)}) copy-start(f32[2,64,4,256]{3,2,1,0:T(4,128)} %param.11) | copy-start | bytes 1572868
  10.2 6.9 copy-start.33
  10.4 144.0 %copy-start.12 = (f32[1,64,4,256]{3,2,1,0:T(4,128)}, f32[1,64,4,256]{3,2,1,0:T(4,128)S(1)}, u32[]{:S(2)}) copy-start(f32[1,64,4,256]{3,2,1,0:T(4,128)S(1)} %sqrt_multiply_fusion.1) | copy-start | bytes 786436
  17.2 3.5 copy-start.18
  20.7 133.8 %copy-start.5 = (f32[1,64,4,256]{3,2,1,0:T(4,128)}, f32[1,64,4,256]{3,2,1,0:T(4,128)S(1)}, u32[]{:S(2)}) copy-start(f32[1,64,4,256]{3,2,1,0:T(4,128)S(1)} %get-tuple-element.83) | copy-start | bytes 786436
  20.7 133.8 %copy-start.7 = (f32[1,64,4,256]{3,2,1,0:T(4,128)}, f32[1,64,4,256]{3,2,1,0:T(4,128)S(1)}, u32[]{:S(2)}) copy-start(f32[1,64,4,256]{3,2,1,0:T(4,128)S(1)} %get-tuple-element.84) | copy-start | bytes 786436
  20.7 141.9 %copy-start.3 = (f32[1,64,4,256]{3,2,1,0:T(4,128)}, f32[1,64,4,256]{3,2,1,0:T(4,128)S(1)}, u32[]{:S(2)}) copy-start(f32[1,64,4,256]{3,2,1,0:T(4,128)S(1)} %get-tuple-element.118) | copy-start | bytes 786436
  22.7 30.3 %all-to-all-start = ((f32[1,2,64,4,256]{4,1,3,0,2:T(2,128)}), f32[1,2,64,4,256]{4,1,3,0,2:T(2,128)}, u32[]{:S(2)}, u32[]{:S(2)}) async-start(f32[1,2,64,4,256]{4,1,3,0,2:T(2,128)} %copy.363), calls=%async_computation | async-start | bytes 1048576 | tf_op jit(solution)/shard_map/all_to_all | solution.py:82
  64.9 87.1 %all-to-all-start.1 = ((f32[1,2,1,256,256]{4,1,2,0,3:T(2,128)}), f32[1,2,1,256,256]{4,1,2,0,3:T(2,128)}, u32[]{:S(2)}, u32[]{:S(2)}) async-start(f32[1,2,1,256,256]{4,1,2,0,3:T(2,128)} %copy.367), calls=%async_computation.1 | async-start | bytes 1048576 | tf_op jit(solution)/shard_map/all_to_all | solution.py:91
  153.9 1.0 copy-start.31
  154.4 9.3 %copy-start.2 = (f32[1,4,256,2,64]{2,0,1,4,3:T(1,128)}, f32[1,4,256,2,64]{2,0,1,4,3:T(1,128)S(1)}, u32[]{:S(2)}) copy-start(f32[1,4,256,2,64]{2,0,1,4,3:T(1,128)S(1)} %copy.761) | copy-start | bytes 1572868
  162.6 0.8 copy-start.24
  199.8 6.2 copy-start.25
  199.8 23.7 %all-to-all-start.3 = ((f32[1,2,1,256,256]{4,1,2,0,3:T(2,128)}), f32[1,2,1,256,256]{4,1,2,0,3:T(2,128)}, u32[]{:S(2)}, u32[]{:S(2)}) async-start(f32[1,2,1,256,256]{4,1,2,0,3:T(2,128)} %copy.384), calls=%async_computation.3 | async-start | bytes 1048576 | tf_op jit(solution)/shard_map/all_to_all | solution.py:91
  206.1 1.0 copy-start.23
  207.0 16.5 %copy-start.14 = (f32[1,64,2,64]{3,1,2,0:T(8,128)S(1)}, f32[1,64,2,64]{3,1,2,0:T(8,128)}, u32[]{:S(2)}) copy-start(f32[1,64,2,64]{3,1,2,0:T(8,128)} %get-tuple-element.128) | copy-start | bytes 98308
  207.0 16.5 %copy-start.16 = (f32[1,64,2,64]{3,1,2,0:T(8,128)S(1)}, f32[1,64,2,64]{3,1,2,0:T(8,128)}, u32[]{:S(2)}) copy-start(f32[1,64,2,64]{3,1,2,0:T(8,128)} %get-tuple-element.129) | copy-start | bytes 98308
  223.5 1.9 copy-start.38
  223.5 1.9 copy-start.40
  263.2 23.6 %all-to-all-start.5 = ((f32[1,2,1,256,256]{4,1,2,0,3:T(2,128)}), f32[1,2,1,256,256]{4,1,2,0,3:T(2,128)}, u32[]{:S(2)}, u32[]{:S(2)}) async-start(f32[1,2,1,256,256]{4,1,2,0,3:T(2,128)} %copy.392), calls=%async_computation.5 | async-start | bytes 1048576 | tf_op jit(solution)/shard_map/all_to_all | solution.py:91
  269.3 152.4 %all-reduce.10.cloned.1.call-start = ((), (), s32[]{:S(2)}) async-start(), calls=%async_computation.11 | async-start | bytes 1572864 | tf_op jit(solution)/shard_map/psum | solution.py:187
  289.1 1.0 copy-start.4
  289.1 1.0 copy-start.42
  289.2 1.1 copy-start.43
  366.8 1.3 copy-start.6
  366.8 1.3 copy-start.8
  368.1 0.8 copy-start
  369.6 3.2 copy-start.19
  422.9 0.8 copy-start.9
  423.7 0.8 copy-start.35
  508.5 0.8 copy-start.29
  508.5 1.1 copy-start.10
  547.4 6.2 copy-start.21
  547.4 23.7 %all-to-all-start.7 = ((f32[1,2,1,256,256]{4,1,2,0,3:T(2,128)}), f32[1,2,1,256,256]{4,1,2,0,3:T(2,128)}, u32[]{:S(2)}, u32[]{:S(2)}) async-start(f32[1,2,1,256,256]{4,1,2,0,3:T(2,128)} %copy.431), calls=%async_computation.7 | async-start | bytes 1048576 | tf_op jit(solution)/shard_map/all_to_all | solution.py:91
  553.7 1.0 copy-start.30
  554.6 16.5 %copy-start.15 = (f32[1,64,2,64]{3,1,2,0:T(8,128)S(1)}, f32[1,64,2,64]{3,1,2,0:T(8,128)}, u32[]{:S(2)}) copy-start(f32[1,64,2,64]{3,1,2,0:T(8,128)} %get-tuple-element.128) | copy-start | bytes 98308
  554.6 16.5 %copy-start.17 = (f32[1,64,2,64]{3,1,2,0:T(8,128)S(1)}, f32[1,64,2,64]{3,1,2,0:T(8,128)}, u32[]{:S(2)}) copy-start(f32[1,64,2,64]{3,1,2,0:T(8,128)} %get-tuple-element.129) | copy-start | bytes 98308
  571.1 1.9 copy-start.39
  571.1 1.9 copy-start.41
  609.8 23.5 %all-to-all-start.9 = ((f32[1,2,1,256,256]{4,1,2,0,3:T(2,128)}), f32[1,2,1,256,256]{4,1,2,0,3:T(2,128)S(1)}, u32[]{:S(2)}, u32[]{:S(2)}) async-start(f32[1,2,1,256,256]{4,1,2,0,3:T(2,128)} %copy.439), calls=%async_computation.9 | async-start | bytes 1048576 | tf_op jit(solution)/shard_map/all_to_all | solution.py:91
  615.7 157.4 %all-reduce.8.cloned.1.call-start = ((), (), s32[]{:S(2)}) async-start(), calls=%async_computation.10 | async-start | bytes 1572864 | tf_op jit(solution)/shard_map/psum | solution.py:187
  635.0 1.0 copy-start.11
  635.0 1.0 copy-start.28
  712.7 1.0 copy-start.1
  716.7 1.0 copy-start.37
  717.7 0.9 copy-start.13
  717.7 1.1 copy-start.32
  773.1 1.7 copy-start.45
  (9 other events, 6.4 us)
Sparse Core Ops, SparseCore 0:
  376.2 45.4 all-reduce.9
  727.5 45.4 all-reduce.7
where the time goes:
time: 790 us; the launch traced here: 783 us
  blocking collectives  398 us (50%)
  waiting for transfers between devices  168 us (21%)
  other arithmetic  58.6 us (7%)
  local copies, waits for them, and re-layouts  46.7 us (6%)
  matrix products  45.3 us (6%)
  starting transfers between devices  43.6 us (6%)
  between operations  22.5 us (3%)
    psum x2, blocking collectives, on_device(): lax.psum((data_local, object_local), ('src', 'space'))  152 us
    psum x2, blocking collectives, descent_total(): return lax.psum(local_sum, ('src', 'space'))  146 us
    all_to_all x4, blocking collectives, transform(): lax.all_to_all(depth_done, 'space', split_axis=2, concat_axis=3, tiled=True)  101 us
    psum x2, waiting for transfers between devices, on_device(): numerator_all, power_all = lax.psum((numerator, power_sum), 'src')  90.3 us
    all_to_all x5, waiting for transfers between devices, transform(): lax.all_to_all(returned, 'space', split_axis=3, concat_axis=2, tiled=True)  65 us
    dot_general x30, matrix products, apply_table(): return jnp.einsum(pattern, table, fields, precision=lax.Precision.HIGHEST)  45.3 us
    all_to_all x5, starting transfers between devices, transform(): lax.all_to_all(returned, 'space', split_axis=3, concat_axis=2, tiled=True)  30.5 us
  transfers between devices with their start and end apart: 8, of which 7 were waited for; matrix products, arithmetic and copies ran while one was open for 2% of the time, Pallas kernels for 0%

commit v1 on v0

--- a/solution.py
+++ b/solution.py
@@ -145,7 +145,7 @@
         chi_inc_real = chi_real * inc_real - chi_imag * inc_imag
         chi_inc_imag = chi_real * inc_imag + chi_imag * inc_real
         object_local = jnp.sum(chi_inc_real * chi_inc_real + chi_inc_imag * chi_inc_imag)
-        data_total, object_total = lax.psum((data_local, object_local), ("src", "space"))
+        data_total, object_total = lax.psum(lax.psum((data_local, object_local), "space"), "src")
         data_weight = 1.0 / data_total
         object_weight = 1.0 / object_total
         total_real = inc_real + scattered[:, 0]

time: 790 us -> 916 us (1.16)
  blocking collectives: 398 us -> 523 us
    psum x2 -> x4, blocking collectives: 152 us -> 270 us  [the longest x2 248 us: on_device(): lax.psum((data_local, object_local), 'space')]
  transfers between devices with their start and end apart: 8 -> 8, of which waited for: 7 -> 7; matrix products, arithmetic and copies ran while one was open for 2% -> 1% of each run, Pallas kernels for 0% -> 0%
where the time goes in v1:
time: 916 us; the launch traced here: 909 us
  blocking collectives  523 us (57%)
  waiting for transfers between devices  168 us (18%)
  other arithmetic  60.3 us (7%)
  local copies, waits for them, and re-layouts  46 us (5%)
  matrix products  45.4 us (5%)
  starting transfers between devices  43.5 us (5%)
  between operations  22.5 us (2%)
    psum x2, blocking collectives, on_device(): lax.psum((data_local, object_local), 'space')  248 us
    psum x2, blocking collectives, descent_total(): return lax.psum(local_sum, ('src', 'space'))  147 us
    all_to_all x4, blocking collectives, transform(): lax.all_to_all(depth_done, 'space', split_axis=2, concat_axis=3, tiled=True)  107 us
    psum x2, waiting for transfers between devices, on_device(): numerator_all, power_all = lax.psum((numerator, power_sum), 'src')  90.3 us
    all_to_all x5, waiting for transfers between devices, transform(): lax.all_to_all(returned, 'space', split_axis=3, concat_axis=2, tiled=True)  65 us
    dot_general x30, matrix products, apply_table(): return jnp.einsum(pattern, table, fields, precision=lax.Precision.HIGHEST)  45.4 us
    all_to_all x5, starting transfers between devices, transform(): lax.all_to_all(returned, 'space', split_axis=3, concat_axis=2, tiled=True)  30.5 us
    psum x2, blocking collectives, on_device(): lax.psum(lax.psum((data_local, object_local), 'space'), 'src')  21.8 us
  transfers between devices with their start and end apart: 8, of which 7 were waited for; matrix products, arithmetic and copies ran while one was open for 1% of the time, Pallas kernels for 0%

profile of v1, /device:TPU:8, one launch (start us, length us, event | category | flops | bytes accessed | tf_op | source)
XLA Modules:
  0.0 909.3 jit_solution(5066509298838068777)
XLA Ops:
  10.4 6.7 copy_cosine_fusion
  17.2 3.5 add_reduce_fusion.1
  22.6 13.0 %all-to-all-start = ((f32[1,2,64,4,256]{4,1,3,0,2:T(2,128)}), f32[1,2,64,4,256]{4,1,3,0,2:T(2,128)}, u32[]{:S(2)}, u32[]{:S(2)}) async-start(f32[1,2,64,4,256]{4,1,3,0,2:T(2,128)} %copy.363), calls=%async_computation | async-start | bytes 1048576 | tf_op jit(solution)/shard_map/all_to_all | solution.py:82
  40.0 12.9 %all-to-all-done = f32[1,2,64,4,256]{4,1,3,0,2:T(2,128)} async-done(((f32[1,2,64,4,256]{4,1,3,0,2:T(2,128)}), f32[1,2,64,4,256]{4,1,3,0,2:T(2,128)}, u32[]{:S(2)}, u32[]{:S(2)}) %all-to-all-start) | async-done | bytes 524320 | tf_op jit(solution)/shard_map/all_to_all | solution.py:82
  52.9 2.0 copy.364
  55.0 2.1 convolution_bitcast_fusion.28
  57.1 1.9 convolution_bitcast_fusion.27
  60.2 2.7 convolution_bitcast_fusion.25
  62.9 2.0 copy.367
  64.9 6.1 all-to-all-start.1
  71.0 2.0 fusion.119
  72.9 125.4 %all-reduce.2 = (f32[]{:T(128)}, f32[]{:T(128)}) all-reduce(f32[]{:T(128)} %get-tuple-element.84, f32[]{:T(128)} %get-tuple-element.135), channel_id=1, replica_groups=mesh['src'=4,'space'=64] {'space'}, use_global_device_ids=true, to_apply=%region_1.2 | all-reduce | flops 2 | bytes 16 | tf_op jit(solution)/shard_map/psum | solution.py:148
  198.4 11.3 %all-reduce.3 = (f32[]{:T(128)}, f32[]{:T(128)}) all-reduce(f32[]{:T(128)} %get-tuple-element.66, f32[]{:T(128)} %get-tuple-element.67), channel_id=1, replica_groups=mesh['src'=4,'space'=64] {'src'}, use_global_device_ids=true, to_apply=%region_2.3 | all-reduce | flops 2 | bytes 16 | tf_op jit(solution)/shard_map/psum | solution.py:148
  214.7 7.7 add_multiply_fusion.1
  225.7 31.7 %all_to_all.40 = f32[1,2,64,4,256]{4,1,3,0,2:T(2,128)S(1)} all-to-all(f32[1,2,64,4,256]{4,1,3,0,2:T(2,128)S(1)} %copy.380), channel_id=1, replica_groups=mesh['src'=4,'space'=64] {'space'}, dimensions={2} | all-to-all | bytes 1048576 | tf_op jit(solution)/shard_map/all_to_all | solution.py:82
  261.8 1.9 convolution_bitcast_fusion.19
  264.7 6.2 all-to-all-start.3
  272.6 15.7 %all-to-all-done.3 = f32[1,2,1,256,256]{4,1,2,0,3:T(2,128)} async-done(((f32[1,2,1,256,256]{4,1,2,0,3:T(2,128)}), f32[1,2,1,256,256]{4,1,2,0,3:T(2,128)}, u32[]{:S(2)}, u32[]{:S(2)}) %all-to-all-start.3) | async-done | bytes 524320 | tf_op jit(solution)/shard_map/all_to_all | solution.py:91
  292.4 23.5 %all_to_all.41 = f32[1,2,64,4,256]{4,1,3,0,2:T(2,128)} all-to-all(f32[1,2,64,4,256]{4,1,3,0,2:T(2,128)S(1)} %copy.388), channel_id=1, replica_groups=mesh['src'=4,'space'=64] {'space'}, dimensions={2} | all-to-all | bytes 1048576 | tf_op jit(solution)/shard_map/all_to_all | solution.py:82
  315.9 2.0 copy.389
  318.0 2.1 convolution_bitcast_fusion.16
  320.1 1.9 convolution_bitcast_fusion.15
  323.2 2.7 convolution_bitcast_fusion.13
  325.9 2.0 copy.392
  327.9 6.1 all-to-all-start.5
  334.9 16.6 %all-to-all-done.5 = f32[1,2,1,256,256]{4,1,2,0,3:T(2,128)} async-done(((f32[1,2,1,256,256]{4,1,2,0,3:T(2,128)}), f32[1,2,1,256,256]{4,1,2,0,3:T(2,128)}, u32[]{:S(2)}, u32[]{:S(2)}) %all-to-all-start.5) | async-done | bytes 524320 | tf_op jit(solution)/shard_map/all_to_all | solution.py:91
  356.4 73.4 %all-reduce.1 = (f32[]{:T(128)}, f32[]{:T(128)}, f32[]{:T(128)}) all-reduce(f32[]{:T(128)} %get-tuple-element.79, f32[]{:T(128)} %fusion.95, f32[]{:T(128)} %fusion.62), channel_id=1, replica_groups=mesh['src'=4,'space'=64] {'src','space'}, use_global_device_ids=true, to_apply=%region_7.8 | all-reduce | flops 3 | bytes 24 | tf_op jit(solution)/shard_map/psum | solution.py:98
  434.6 3.2 fusion.56
  437.8 2.3 fusion.49
  441.0 45.6 %all-reduce.11.cloned.1.call-done = (f32[2,64,4,256]{3,2,1,0:T(4,128)}, f32[64,4,256]{2,1,0:T(4,128)}) async-done(((f32[2,64,4,256]{3,2,1,0:T(4,128)}, f32[64,4,256]{2,1,0:T(4,128)}), (f32[2,64,4,256]{3,2,1,0:T(4,128)}, f32[64,4,256]{2,1,0:T(4,128)})) %all-reduce.11.cloned.1.call-update) | async-done | bytes 786448 | tf_op jit(solution)/shard_map/psum | solution.py:187
  489.4 4.4 add_reduce_fusion
  493.8 122.8 %psum.127 = f32[]{:T(128)} all-reduce(f32[]{:T(128)} %add_reduce_fusion), channel_id=1, replica_groups=mesh['src'=4,'space'=64] {'space'}, use_global_device_ids=true, to_apply=%region_15.16 | all-reduce | flops 1 | bytes 8 | tf_op jit(solution)/shard_map/psum | solution.py:148
  617.9 10.5 %psum.128 = f32[]{:T(128)} all-reduce(f32[]{:T(128)} %psum.127), channel_id=1, replica_groups=mesh['src'=4,'space'=64] {'src'}, use_global_device_ids=true, to_apply=%region_16.17 | all-reduce | flops 1 | bytes 8 | tf_op jit(solution)/shard_map/psum | solution.py:148
  629.1 4.0 add_multiply_fusion
  637.3 27.9 %all_to_all.42 = f32[1,2,64,4,256]{4,1,3,0,2:T(2,128)} all-to-all(f32[1,2,64,4,256]{4,1,3,0,2:T(2,128)S(1)} %copy.427), channel_id=1, replica_groups=mesh['src'=4,'space'=64] {'space'}, dimensions={2} | all-to-all | bytes 1048576 | tf_op jit(solution)/shard_map/all_to_all | solution.py:82
  673.5 6.2 all-to-all-start.7
  681.7 15.5 %all-to-all-done.7 = f32[1,2,1,256,256]{4,1,2,0,3:T(2,128)} async-done(((f32[1,2,1,256,256]{4,1,2,0,3:T(2,128)}), f32[1,2,1,256,256]{4,1,2,0,3:T(2,128)}, u32[]{:S(2)}, u32[]{:S(2)}) %all-to-all-start.7) | async-done | bytes 524320 | tf_op jit(solution)/shard_map/all_to_all | solution.py:91
  702.0 23.5 %all_to_all.43 = f32[1,2,64,4,256]{4,1,3,0,2:T(2,128)} all-to-all(f32[1,2,64,4,256]{4,1,3,0,2:T(2,128)S(1)} %copy.435), channel_id=1, replica_groups=mesh['src'=4,'space'=64] {'space'}, dimensions={2} | all-to-all | bytes 1048576 | tf_op jit(solution)/shard_map/all_to_all | solution.py:82
  725.5 2.0 copy.436
  727.6 2.1 convolution_bitcast_fusion.4
  729.7 1.9 convolution_bitcast_fusion.3
  732.8 1.9 convolution_bitcast_fusion.1
  735.7 5.9 all-to-all-start.9
  742.0 17.1 %all-to-all-done.9 = f32[1,2,1,256,256]{4,1,2,0,3:T(2,128)S(1)} async-done(((f32[1,2,1,256,256]{4,1,2,0,3:T(2,128)}), f32[1,2,1,256,256]{4,1,2,0,3:T(2,128)S(1)}, u32[]{:S(2)}, u32[]{:S(2)}) %all-to-all-start.9) | async-done | bytes 524320 | tf_op jit(solution)/shard_map/all_to_all | solution.py:91
  762.7 73.2 %all-reduce = (f32[]{:T(128)}, f32[]{:T(128)}, f32[]{:T(128)}) all-reduce(f32[]{:T(128)} %get-tuple-element.74, f32[]{:T(128)} %fusion.96, f32[]{:T(128)} %fusion.44), channel_id=1, replica_groups=mesh['src'=4,'space'=64] {'src','space'}, use_global_device_ids=true, to_apply=%region_18.19 | all-reduce | flops 3 | bytes 24 | tf_op jit(solution)/shard_map/psum | solution.py:98
  840.5 2.1 fusion.41
  844.6 7.3 multiply_add_fusion.1
  854.2 44.7 %all-reduce.9.cloned.1.call-done = (f32[2,64,4,256]{3,0,2,1:T(2,128)}, f32[64,4,256]{2,0,1:T(8,128)}) async-done(((f32[2,64,4,256]{3,0,2,1:T(2,128)}, f32[64,4,256]{2,0,1:T(8,128)}), (f32[2,64,4,256]{3,0,2,1:T(2,128)}, f32[64,4,256]{2,0,1:T(8,128)})) %all-reduce.9.cloned.1.call-update) | async-done | bytes 786448 | tf_op jit(solution)/shard_map/psum | solution.py:187
  (210 shorter events, 77.6 us)
Async XLA Ops:
  7.2 10.0 %copy-start.43 = (f32[2,64,4,256]{3,2,1,0:T(4,128)S(1)}, f32[2,64,4,256]{3,2,1,0:T(4,128)}, u32[]{:S(2)}) copy-start(f32[2,64,4,256]{3,2,1,0:T(4,128)} %param.11) | copy-start | bytes 1572868
  10.2 6.9 copy-start.32
  10.4 203.9 %copy-start.12 = (f32[1,64,4,256]{3,2,1,0:T(4,128)}, f32[1,64,4,256]{3,2,1,0:T(4,128)S(1)}, u32[]{:S(2)}) copy-start(f32[1,64,4,256]{3,2,1,0:T(4,128)S(1)} %sqrt_multiply_fusion.1) | copy-start | bytes 786436
  17.2 3.5 copy-start.18
  20.6 193.7 %copy-start.5 = (f32[1,64,4,256]{3,2,1,0:T(4,128)}, f32[1,64,4,256]{3,2,1,0:T(4,128)S(1)}, u32[]{:S(2)}) copy-start(f32[1,64,4,256]{3,2,1,0:T(4,128)S(1)} %get-tuple-element.85) | copy-start | bytes 786436
  20.6 193.7 %copy-start.7 = (f32[1,64,4,256]{3,2,1,0:T(4,128)}, f32[1,64,4,256]{3,2,1,0:T(4,128)S(1)}, u32[]{:S(2)}) copy-start(f32[1,64,4,256]{3,2,1,0:T(4,128)S(1)} %get-tuple-element.86) | copy-start | bytes 786436
  20.6 201.9 %copy-start.3 = (f32[1,64,4,256]{3,2,1,0:T(4,128)}, f32[1,64,4,256]{3,2,1,0:T(4,128)S(1)}, u32[]{:S(2)}) copy-start(f32[1,64,4,256]{3,2,1,0:T(4,128)S(1)} %get-tuple-element.120) | copy-start | bytes 786436
  22.6 30.3 %all-to-all-start = ((f32[1,2,64,4,256]{4,1,3,0,2:T(2,128)}), f32[1,2,64,4,256]{4,1,3,0,2:T(2,128)}, u32[]{:S(2)}, u32[]{:S(2)}) async-start(f32[1,2,64,4,256]{4,1,3,0,2:T(2,128)} %copy.363), calls=%async_computation | async-start | bytes 1048576 | tf_op jit(solution)/shard_map/all_to_all | solution.py:82
  64.9 147.0 %all-to-all-start.1 = ((f32[1,2,1,256,256]{4,1,2,0,3:T(2,128)}), f32[1,2,1,256,256]{4,1,2,0,3:T(2,128)}, u32[]{:S(2)}, u32[]{:S(2)}) async-start(f32[1,2,1,256,256]{4,1,2,0,3:T(2,128)} %copy.367), calls=%async_computation.1 | async-start | bytes 1048576 | tf_op jit(solution)/shard_map/all_to_all | solution.py:91
  213.8 1.0 copy-start.30
  214.3 9.3 %copy-start.2 = (f32[1,4,256,2,64]{2,0,1,4,3:T(1,128)}, f32[1,4,256,2,64]{2,0,1,4,3:T(1,128)S(1)}, u32[]{:S(2)}) copy-start(f32[1,4,256,2,64]{2,0,1,4,3:T(1,128)S(1)} %copy.761) | copy-start | bytes 1572868
  222.5 0.8 copy-start.24
  264.7 6.2 copy-start.25
  264.7 23.7 %all-to-all-start.3 = ((f32[1,2,1,256,256]{4,1,2,0,3:T(2,128)}), f32[1,2,1,256,256]{4,1,2,0,3:T(2,128)}, u32[]{:S(2)}, u32[]{:S(2)}) async-start(f32[1,2,1,256,256]{4,1,2,0,3:T(2,128)} %copy.384), calls=%async_computation.3 | async-start | bytes 1048576 | tf_op jit(solution)/shard_map/all_to_all | solution.py:91
  270.9 1.0 copy-start.23
  271.9 16.5 %copy-start.14 = (f32[1,64,2,64]{3,1,2,0:T(8,128)S(1)}, f32[1,64,2,64]{3,1,2,0:T(8,128)}, u32[]{:S(2)}) copy-start(f32[1,64,2,64]{3,1,2,0:T(8,128)} %get-tuple-element.130) | copy-start | bytes 98308
  271.9 16.5 %copy-start.16 = (f32[1,64,2,64]{3,1,2,0:T(8,128)S(1)}, f32[1,64,2,64]{3,1,2,0:T(8,128)}, u32[]{:S(2)}) copy-start(f32[1,64,2,64]{3,1,2,0:T(8,128)} %get-tuple-element.131) | copy-start | bytes 98308
  288.4 1.9 copy-start.37
  288.4 1.9 copy-start.39
  327.9 23.6 %all-to-all-start.5 = ((f32[1,2,1,256,256]{4,1,2,0,3:T(2,128)}), f32[1,2,1,256,256]{4,1,2,0,3:T(2,128)}, u32[]{:S(2)}, u32[]{:S(2)}) async-start(f32[1,2,1,256,256]{4,1,2,0,3:T(2,128)} %copy.392), calls=%async_computation.5 | async-start | bytes 1048576 | tf_op jit(solution)/shard_map/all_to_all | solution.py:91
  334.0 152.6 %all-reduce.11.cloned.1.call-start = ((), (), s32[]{:S(2)}) async-start(), calls=%async_computation.11 | async-start | bytes 1572864 | tf_op jit(solution)/shard_map/psum | solution.py:187
  353.8 1.0 copy-start.4
  353.9 1.0 copy-start.41
  353.9 1.1 copy-start.42
  431.7 1.3 copy-start.6
  431.7 1.3 copy-start.8
  433.0 0.8 copy-start
  434.6 3.2 copy-start.19
  487.9 0.8 copy-start.9
  488.7 0.8 copy-start.34
  633.0 0.8 copy-start.28
  633.0 1.1 copy-start.10
  673.5 6.2 copy-start.21
  673.5 23.7 %all-to-all-start.7 = ((f32[1,2,1,256,256]{4,1,2,0,3:T(2,128)}), f32[1,2,1,256,256]{4,1,2,0,3:T(2,128)}, u32[]{:S(2)}, u32[]{:S(2)}) async-start(f32[1,2,1,256,256]{4,1,2,0,3:T(2,128)} %copy.431), calls=%async_computation.7 | async-start | bytes 1048576 | tf_op jit(solution)/shard_map/all_to_all | solution.py:91
  679.7 1.0 copy-start.29
  680.7 16.5 %copy-start.15 = (f32[1,64,2,64]{3,1,2,0:T(8,128)S(1)}, f32[1,64,2,64]{3,1,2,0:T(8,128)}, u32[]{:S(2)}) copy-start(f32[1,64,2,64]{3,1,2,0:T(8,128)} %get-tuple-element.130) | copy-start | bytes 98308
  680.7 16.5 %copy-start.17 = (f32[1,64,2,64]{3,1,2,0:T(8,128)S(1)}, f32[1,64,2,64]{3,1,2,0:T(8,128)}, u32[]{:S(2)}) copy-start(f32[1,64,2,64]{3,1,2,0:T(8,128)} %get-tuple-element.131) | copy-start | bytes 98308
  697.2 1.9 copy-start.38
  697.2 1.9 copy-start.40
  735.7 23.4 %all-to-all-start.9 = ((f32[1,2,1,256,256]{4,1,2,0,3:T(2,128)}), f32[1,2,1,256,256]{4,1,2,0,3:T(2,128)S(1)}, u32[]{:S(2)}, u32[]{:S(2)}) async-start(f32[1,2,1,256,256]{4,1,2,0,3:T(2,128)} %copy.439), calls=%async_computation.9 | async-start | bytes 1048576 | tf_op jit(solution)/shard_map/all_to_all | solution.py:91
  741.6 157.3 %all-reduce.9.cloned.1.call-start = ((), (), s32[]{:S(2)}) async-start(), calls=%async_computation.10 | async-start | bytes 1572864 | tf_op jit(solution)/shard_map/psum | solution.py:187
  760.9 1.0 copy-start.11
  760.9 1.0 copy-start.27
  838.5 1.0 copy-start.1
  842.6 1.0 copy-start.36
  843.5 0.9 copy-start.13
  843.5 1.1 copy-start.31
  898.9 1.7 copy-start.44
  (8 other events, 5.7 us)
Sparse Core Ops, SparseCore 0:
  441.1 45.4 all-reduce.10
  853.4 45.4 all-reduce.8
